TPU v7x, 256 devices: a whole 4x4x8 slice. The times are simulated.
256 devices in a mesh: box: 32 (over y_hi, z, core), dir: 8 (over y_lo, x).
Axes of the slice: x: 4, y: 4 (y_hi: 2, y_lo: 2; y = y_hi * 2 + y_lo), z: 8, core: 2. Of those that a mesh axis runs over, the one named last changes fastest.
Arguments:
- leaf_density: bfloat16 [2048, 96, 8, 128], P('box', 'dir'), may hold values from -6 to 6
- phases_first: float32 [8, 96, 64], P(None, 'dir'), may hold values from -3.140625 to 3.140625
- phases_switch: float32 [8, 384, 64], P(None, 'dir'), may hold values from -3.140625 to 3.140625
- phases_top: float32 [8, 1536, 64], P(None, ('box', 'dir')), may hold values from -3.140625 to 3.140625
- transfer_first: bfloat16 [96, 2, 64, 512], P('dir'), may hold values from -0.1875 to 0.1875
- transfer_switch: bfloat16 [384, 2, 64, 512], P('dir'), may hold values from -0.1875 to 0.1875
- transfer_top: bfloat16 [1536, 2, 64, 512], P(('box', 'dir')), may hold values from -0.1875 to 0.1875
- child_mid: int32 [384], P('dir'), may hold values from 0 to 95, as said below
- child_top: int32 [1536], replicated, may hold values from 0 to 383, as said below
Outputs:
- top_density: float32 [4, 1536, 8, 128], P(None, ('box', 'dir'))
Inputs may be any that keep to these rules, and one draw needn't show every extreme that they name: `child_mid`: each level-1 wedge contains exactly 4 level-2 wedges. Each level-2 wedge contains exactly 4 level-3 wedges; with j = (w // 6) mod 8, child_top[w] lies in the level-2 wedges j * 48 to (j + 1) * 48 - 1.
All inputs are finite; a program needn't handle non-finite values.
Results may differ from a plain program's by a relative error of at most 0.0064.
Values may be sent and summed in bfloat16 or wider, within the bound.
No kernel may reach another device: no remote copies, remote signals or barrier semaphores. Data moves between devices by JAX's collectives and lax.ppermute only.
A program may use at most 64 MiB of HBM per device.

v0:
```python
import jax
import jax.numpy as jnp
from jax import lax
from jax.sharding import PartitionSpec as P


def lift_level(density, angles, transfer):
    box_count, wedges, excite, full_width = density.shape
    half_width = full_width // 2
    parents = box_count // 8
    children = density.reshape(parents, 8, wedges, excite, full_width).astype(jnp.float32)
    real_part = children[..., :half_width]
    imag_part = children[..., half_width:]
    cos_part = jnp.cos(angles)[None, :, :, None, :]
    sine_part = jnp.sin(angles)[None, :, :, None, :]
    phased = jnp.stack(
        [
            cos_part * real_part - sine_part * imag_part,
            sine_part * real_part + cos_part * imag_part,
        ],
        axis=4,
    ).astype(jnp.bfloat16)
    blocks = transfer.reshape(wedges, 2, half_width, 8, half_width)
    product = jnp.einsum("pcwnsr,wtkcr->pwnstk", phased, blocks, preferred_element_type=jnp.float32)
    real_out = product[..., 0, 0, :] - product[..., 1, 1, :]
    imag_out = product[..., 1, 0, :] + product[..., 0, 1, :]
    return jnp.concatenate([real_out, imag_out], axis=-1)


def shards(
    leaf_density,
    phases_first,
    phases_switch,
    phases_top,
    transfer_first,
    transfer_switch,
    transfer_top,
    child_mid,
    child_top,
):
    level_one = lift_level(leaf_density, phases_first, transfer_first).astype(jnp.bfloat16)
    all_low = lax.all_gather(level_one, "dir", axis=1, tiled=True)
    selected = jnp.take(all_low, child_mid, axis=1)
    level_two = lift_level(selected, phases_switch, transfer_switch).astype(jnp.bfloat16)
    mid_local = level_two.shape[1]
    top_count = transfer_top.shape[0]
    dir_index = lax.axis_index("dir")
    box_index = lax.axis_index("box")
    dir_count = lax.axis_size("dir")
    share_start = dir_index * mid_local
    every_box = lax.all_gather(level_two, "box", axis=0, tiled=True)
    own_start = (box_index * dir_count + dir_index) * top_count
    own_table = lax.dynamic_slice_in_dim(child_top, own_start, top_count, 0) - share_start
    top_input = jnp.take(every_box, own_table, axis=1)
    return lift_level(top_input, phases_top, transfer_top)


def solution(mesh):
    placed = (
        P("box", "dir", None, None),
        P(None, "dir", None),
        P(None, "dir", None),
        P(None, ("box", "dir"), None),
        P("dir", None, None, None),
        P("dir", None, None, None),
        P(("box", "dir"), None, None, None),
        P("dir"),
        P(),
    )
    return jax.shard_map(
        shards,
        mesh=mesh,
        in_specs=placed,
        out_specs=P(None, ("box", "dir"), None, None),
        check_vma=False,
    )
```

profile of v0, /device:TPU:1, one launch (start us, length us, event | category | flops | bytes accessed | tf_op | source)
XLA Modules:
  0.0 171.6 jit_solution(9915890975607049855)
XLA Ops:
  6.5 0.0 all-gather.3.cloned.1.call-start
  6.5 1.0 fusion.45
  7.5 1.7 copy.27
  9.2 5.2 %reshape.133 = bf16[12,2,64,8,64]{4,3,2,1,0:T(8,128)(2,1)} reshape(bf16[12,2,64,512]{3,2,1,0:T(8,128)(2,1)} %param.13) | data formatting | bytes 3145728 | tf_op jit(solution)/shard_map/reshape | solution.py:23
  14.4 0.0 copy-start
  14.4 1.2 fusion.6
  15.5 0.7 copy-done
  16.2 1.6 fusion.12
  17.9 0.0 copy-start.2
  17.9 0.1 fusion.31
  17.9 0.1 fusion.32
  18.0 0.8 pad_maximum_fusion
  18.8 0.0 all-gather.3.cloned.1.call-update
  18.9 0.0 all-gather.5.cloned.1.call-start
  18.9 0.0 copy-done.2
  18.9 0.7 fusion.44
  19.6 0.1 copy.26
  19.7 0.1 copy.32
  19.8 0.0 copy-start.4
  19.8 16.3 %reshape.134 = bf16[48,2,64,8,64]{4,3,2,1,0:T(8,128)(2,1)} reshape(bf16[48,2,64,512]{3,2,1,0:T(8,128)(2,1)} %param.14) | data formatting | bytes 12582912 | tf_op jit(solution)/shard_map/reshape | solution.py:23
  36.0 0.0 copy-done.4
  36.1 23.9 %all-gather.3.cloned.1.call-done = bf16[8,96,8,128]{3,2,0,1:T(8,128)(2,1)} async-done(((bf16[8,12,8,128]{3,2,0,1:T(8,128)(2,1)}), bf16[8,96,8,128]{3,2,0,1:T(8,128)(2,1)}) %all-gather.3.cloned.1.call-update) | async-done | bytes 1572880 | tf_op jit(solution)/shard_map/all_gather | solution.py:42
  60.0 2.1 %gather_fusion = bf16[48,8,8,128]{3,2,1,0:T(8,128)(2,1)S(1)} fusion(bf16[8,96,8,128]{3,2,0,1:T(8,128)(2,1)} %all-gather.3.cloned.1.call-done, s32[1024]{0:T(1024)S(1)} %pad_clamp_fusion.1), kind=kCustom, calls=%fused_computation | custom fusion | bytes 1573056 | tf_op jit(solution)/shard_map/jit(_take)/gather | solution.py:43
  62.1 0.2 fusion.25
  62.3 0.7 fusion.21
  63.0 7.9 %fusion.15 = f32[1,48,8,2,2,64]{5,2,4,3,1,0:T(8,128)S(1)} fusion(bf16[48,2,64,8,64,1]{4,3,2,1,0,5:T(8,128)(2,1)} %bitcast.126, bf16[8,48,8,1,64]{4,2,0,3,1:T(8,128)(2,1)S(1)} %get-tuple-element.10, bf16[8,48,8,1,64]{4,2,0,3,1:T(8,128)(2,1)S(1)} %get-tuple-element.9), kind=kOutput, calls=%fused_computation.21 | convolution fusion | flops 102236160 | bytes 7471104 | tf_op jit(solution)/shard_map/pcwnsr,wtkcr->pwnstk/dot_general | solution.py:24
  70.9 0.0 copy-start.1
  71.0 0.0 copy-start.3
  71.0 0.7 pad_maximum_fusion.1
  71.8 0.0 all-gather.5.cloned.1.call-update
  71.8 0.3 copy-done.1
  72.1 0.8 reshape.135
  72.9 0.8 compare_and_fusion.1
  73.7 0.0 copy-done.3
  73.7 0.1 fusion.46
  73.8 86.1 %all-gather.5.cloned.1.call-done = bf16[32,48,8,128]{3,2,1,0:T(8,128)(2,1)} async-done(((bf16[1,48,8,128]{3,2,1,0:T(8,128)(2,1)}), bf16[32,48,8,128]{3,2,1,0:T(8,128)(2,1)}) %all-gather.5.cloned.1.call-update) | async-done | bytes 3145744 | tf_op jit(solution)/shard_map/all_gather | solution.py:51
  160.0 2.6 %gather_fusion.1 = bf16[6,32,8,128]{3,2,1,0:T(8,128)(2,1)S(1)} fusion(bf16[32,48,8,128]{3,2,1,0:T(8,128)(2,1)} %all-gather.5.cloned.1.call-done, s32[1024]{0:T(1024)S(1)} %pad_clamp_fusion), kind=kCustom, calls=%fused_computation.1 | custom fusion | bytes 786456 | tf_op jit(solution)/shard_map/jit(_take)/gather | solution.py:54
  162.5 0.1 select_convert_fusion
  162.7 0.4 fusion.26
  163.1 0.9 fusion.18
  164.0 0.1 pad_maximum_fusion.2
  164.1 0.6 copy.41
  (8 shorter events, 0.1 us)
Async XLA Ops:
  6.5 53.5 %all-gather.3.cloned.1.call-start = ((), (), s32[]{:S(2)}) async-start(), calls=%async_computation | async-start | bytes 1769472 | tf_op jit(solution)/shard_map/all_gather | solution.py:42
  14.4 1.9 %copy-start = (bf16[12,2,64,8,64]{4,3,2,1,0:T(8,128)(2,1)S(1)}, bf16[12,2,64,8,64]{4,3,2,1,0:T(8,128)(2,1)}, u32[]{:S(2)}) copy-start(bf16[12,2,64,8,64]{4,3,2,1,0:T(8,128)(2,1)} %reshape.133) | copy-start | bytes 4718596
  17.9 1.0 copy-start.2
  18.9 141.1 %all-gather.5.cloned.1.call-start = ((), (), s32[]{:S(2)}) async-start(), calls=%async_computation.1 | async-start | bytes 3244032 | tf_op jit(solution)/shard_map/all_gather | solution.py:51
  19.8 16.3 %copy-start.4 = (s32[48]{0:T(128)S(1)}, s32[48]{0:T(128)}, u32[]{:S(2)}) copy-start(s32[48]{0:T(128)} %param.16) | copy-start | bytes 580
  70.9 1.2 copy-start.1
  71.0 2.7 %copy-start.3 = (f32[8,6,64]{2,0,1:T(8,128)S(1)}, f32[8,6,64]{2,0,1:T(8,128)}, u32[]{:S(2)}) copy-start(f32[8,6,64]{2,0,1:T(8,128)} %param.12) | copy-start | bytes 36868
Sparse Core Ops, SparseCore 0:
  19.0 40.9 all-gather.2
  71.9 88.0 all-gather.4
where the time goes:
time: 172 us
  waiting for transfers between devices  110 us (64%)
  local copies, waits for them, and re-layouts  32.2 us (19%)
  between operations  13.6 us (8%)
  matrix products  10.4 us (6%)
  other arithmetic  5.25 us (3%)
    all_gather x1, waiting for transfers between devices, shards(): every_box = lax.all_gather(level_two, 'box', axis=0, tiled=True)  86.1 us
    all_gather x1, waiting for transfers between devices, shards(): all_low = lax.all_gather(level_one, 'dir', axis=1, tiled=True)  23.9 us
    reshape x3, local copies, waits for them, and re-layouts, lift_level(): blocks = transfer.reshape(wedges, 2, half_width, 8, half_width)  22.2 us
    dot_general x3, matrix products, lift_level(): jnp.einsum('pcwnsr,wtkcr->pwnstk', phased, blocks, preferred_element_type...  10.4 us
  transfers between devices with their start and end apart: 2, of which 2 were waited for; matrix products, arithmetic and copies ran while one was open for 11% of the time, Pallas kernels for 0%

commit v1 on v0

--- a/solution.py
+++ b/solution.py
@@ -39,7 +39,9 @@
     child_top,
 ):
     level_one = lift_level(leaf_density, phases_first, transfer_first).astype(jnp.bfloat16)
-    all_low = lax.all_gather(level_one, "dir", axis=1, tiled=True)
+    all_low = jnp.concatenate(
+        lax.all_to_all(jnp.stack([level_one] * lax.axis_size("dir")), "dir", 0, 0), axis=1
+    )
     selected = jnp.take(all_low, child_mid, axis=1)
     level_two = lift_level(selected, phases_switch, transfer_switch).astype(jnp.bfloat16)
     mid_local = level_two.shape[1]

time: 172 us -> 154 us (0.90)
  waiting for transfers between devices: 110 us -> 86.4 us
  starting transfers between devices: 0.04 us -> 6.01 us
    all_gather x1 -> x0, waiting for transfers between devices: 23.9 us -> none  [shards(): all_low = lax.all_gather(level_one, 'dir', axis=1, tiled=True)]
    all_to_all x0 -> x1, starting transfers between devices: none -> 5.97 us  [shards(): lax.all_to_all(jnp.stack([level_one] * lax.axis_size('dir')), 'dir', 0, 0)]
    all_to_all x0 -> x1, waiting for transfers between devices: none -> 4.3 us  [shards(): lax.all_to_all(jnp.stack([level_one] * lax.axis_size('dir')), 'dir', 0, 0)]
    all_gather x1, waiting for transfers between devices: 86.1 us -> 82.1 us  [shards(): every_box = lax.all_gather(level_two, 'box', axis=0, tiled=True)]
  transfers between devices with their start and end apart: 2 -> 2, of which waited for: 2 -> 2; matrix products, arithmetic and copies ran while one was open for 11% -> 12% of each run, Pallas kernels for 0% -> 0%
where the time goes in v1:
time: 154 us; the launch traced here: 153 us
  waiting for transfers between devices  86.4 us (56%)
  local copies, waits for them, and re-layouts  32.5 us (21%)
  between operations  13.6 us (9%)
  matrix products  10.4 us (7%)
  starting transfers between devices  6.01 us (4%)
  other arithmetic  4.55 us (3%)
    all_gather x1, waiting for transfers between devices, shards(): every_box = lax.all_gather(level_two, 'box', axis=0, tiled=True)  82.1 us
    reshape x3, local copies, waits for them, and re-layouts, lift_level(): blocks = transfer.reshape(wedges, 2, half_width, 8, half_width)  22.2 us
    dot_general x3, matrix products, lift_level(): jnp.einsum('pcwnsr,wtkcr->pwnstk', phased, blocks, preferred_element_type...  10.4 us
    all_to_all x1, starting transfers between devices, shards(): lax.all_to_all(jnp.stack([level_one] * lax.axis_size('dir')), 'dir', 0, 0)  5.97 us
    all_to_all x1, waiting for transfers between devices, shards(): lax.all_to_all(jnp.stack([level_one] * lax.axis_size('dir')), 'dir', 0, 0)  4.3 us
  transfers between devices with their start and end apart: 2, of which 2 were waited for; matrix products, arithmetic and copies ran while one was open for 12% of the time, Pallas kernels for 0%

profile of v1, /device:TPU:1, one launch (start us, length us, event | category | flops | bytes accessed | tf_op | source)
XLA Modules:
  0.0 153.5 jit_solution(2466601171001001099)
XLA Ops:
  6.5 1.0 fusion.45
  7.5 1.7 %copy.45 = f32[64,12,8,128]{3,2,0,1:T(8,128)S(1)} copy(bf16[64,12,8,128]{3,2,1,0:T(8,128)(2,1)} %param.9) | data formatting | bytes 4718592 | tf_op jit(solution)/shard_map/convert_element_type | solution.py:11
  9.2 5.2 %reshape.146 = bf16[12,2,64,8,64]{4,3,2,1,0:T(8,128)(2,1)} reshape(bf16[12,2,64,512]{3,2,1,0:T(8,128)(2,1)} %param.13) | data formatting | bytes 3145728 | tf_op jit(solution)/shard_map/reshape | solution.py:23
  14.4 0.0 copy-start
  14.4 1.2 fusion.6
  15.6 0.7 copy-done
  16.3 1.6 %fusion.12 = f32[8,12,8,2,2,64]{5,2,4,3,0,1:T(8,128)S(1)} fusion(bf16[12,2,64,8,64,1,1]{4,3,2,1,0,6,5:T(8,128)(2,1)S(1)} %bitcast.131, bf16[8,8,12,8,1,64]{5,3,1,4,0,2:T(8,128)(2,1)S(1)} %get-tuple-element.8, bf16[8,8,12,8,1,64]{5,3,1,4,0,2:T(8,128)(2,1)S(1)} %get-tuple-element.7), kind=kOutput, calls=%fused_computation.20 | convolution fusion | flops 204472320 | bytes 3932160 | tf_op jit(solution)/shard_map/pcwnsr,wtkcr->pwnstk/dot_general | solution.py:24
  17.9 0.1 fusion.31
  17.9 0.1 fusion.32
  18.0 0.1 pad_maximum_fusion
  18.2 1.4 stack.47
  19.6 0.0 copy-start.2
  19.6 6.0 %all-to-all-start = ((bf16[8,8,12,8,128]{4,3,2,1,0:T(8,128)(2,1)}), bf16[8,8,12,8,128]{4,3,2,1,0:T(8,128)(2,1)S(1)}, u32[]{:S(2)}, u32[]{:S(2)}) async-start(bf16[8,8,12,8,128]{4,3,2,1,0:T(8,128)(2,1)} %stack.47), calls=%async_computation | async-start | bytes 3145728 | tf_op jit(solution)/shard_map/all_to_all | solution.py:43
  25.6 0.0 all-gather.2.cloned.1.call-start
  25.7 0.0 copy-done.2
  25.7 0.7 fusion.44
  26.4 0.1 copy.44
  26.4 0.1 copy.52
  26.5 0.0 copy-start.4
  26.5 16.3 %reshape.149 = bf16[48,2,64,8,64]{4,3,2,1,0:T(8,128)(2,1)} reshape(bf16[48,2,64,512]{3,2,1,0:T(8,128)(2,1)} %param.14) | data formatting | bytes 12582912 | tf_op jit(solution)/shard_map/reshape | solution.py:23
  42.8 0.0 copy-done.4
  42.8 4.3 %all-to-all-done = bf16[8,8,12,8,128]{4,3,2,1,0:T(8,128)(2,1)S(1)} async-done(((bf16[8,8,12,8,128]{4,3,2,1,0:T(8,128)(2,1)}), bf16[8,8,12,8,128]{4,3,2,1,0:T(8,128)(2,1)S(1)}, u32[]{:S(2)}, u32[]{:S(2)}) %all-to-all-start) | async-done | bytes 1572896 | tf_op jit(solution)/shard_map/all_to_all | solution.py:43
  47.1 0.1 copy.51
  47.2 0.8 gather_fusion
  48.1 0.2 fusion.25
  48.3 0.7 fusion.21
  49.0 7.9 %fusion.15 = f32[1,48,8,2,2,64]{5,2,4,3,1,0:T(8,128)S(1)} fusion(bf16[48,2,64,8,64,1]{4,3,2,1,0,5:T(8,128)(2,1)} %bitcast.129, bf16[8,48,8,1,64]{4,2,0,3,1:T(8,128)(2,1)S(1)} %get-tuple-element.10, bf16[8,48,8,1,64]{4,2,0,3,1:T(8,128)(2,1)S(1)} %get-tuple-element.9), kind=kOutput, calls=%fused_computation.21 | convolution fusion | flops 102236160 | bytes 7471104 | tf_op jit(solution)/shard_map/pcwnsr,wtkcr->pwnstk/dot_general | solution.py:24
  56.9 0.0 copy-start.1
  56.9 0.0 copy-start.3
  57.0 0.7 pad_maximum_fusion.1
  57.7 0.0 all-gather.2.cloned.1.call-update
  57.8 0.3 copy-done.1
  58.1 0.8 reshape.150
  58.9 0.8 compare_and_fusion.1
  59.7 0.0 copy-done.3
  59.7 0.1 fusion.46
  59.8 82.1 %all-gather.2.cloned.1.call-done = bf16[32,48,8,128]{3,2,1,0:T(8,128)(2,1)} async-done(((bf16[1,48,8,128]{3,2,1,0:T(8,128)(2,1)}), bf16[32,48,8,128]{3,2,1,0:T(8,128)(2,1)}) %all-gather.2.cloned.1.call-update) | async-done | bytes 3145744 | tf_op jit(solution)/shard_map/all_gather | solution.py:53
  141.9 2.6 %gather_fusion.1 = bf16[6,32,8,128]{3,2,1,0:T(8,128)(2,1)S(1)} fusion(bf16[32,48,8,128]{3,2,1,0:T(8,128)(2,1)} %all-gather.2.cloned.1.call-done, s32[1024]{0:T(1024)S(1)} %pad_clamp_fusion), kind=kCustom, calls=%fused_computation.1 | custom fusion | bytes 786456 | tf_op jit(solution)/shard_map/jit(_take)/gather | solution.py:56
  144.5 0.1 select_convert_fusion
  144.6 0.4 fusion.26
  145.0 0.9 fusion.18
  145.9 0.1 pad_maximum_fusion.2
  146.0 0.6 copy.61
  (9 shorter events, 0.2 us)
Async XLA Ops:
  14.4 1.9 %copy-start = (bf16[12,2,64,8,64]{4,3,2,1,0:T(8,128)(2,1)S(1)}, bf16[12,2,64,8,64]{4,3,2,1,0:T(8,128)(2,1)}, u32[]{:S(2)}) copy-start(bf16[12,2,64,8,64]{4,3,2,1,0:T(8,128)(2,1)} %reshape.146) | copy-start | bytes 4718596
  19.6 6.0 %copy-start.2 = (f32[8,48,64]{2,1,0:T(8,128)S(1)}, f32[8,48,64]{2,1,0:T(8,128)}, u32[]{:S(2)}) copy-start(f32[8,48,64]{2,1,0:T(8,128)} %param.11) | copy-start | bytes 294916
  19.6 27.5 %all-to-all-start = ((bf16[8,8,12,8,128]{4,3,2,1,0:T(8,128)(2,1)}), bf16[8,8,12,8,128]{4,3,2,1,0:T(8,128)(2,1)S(1)}, u32[]{:S(2)}, u32[]{:S(2)}) async-start(bf16[8,8,12,8,128]{4,3,2,1,0:T(8,128)(2,1)} %stack.47), calls=%async_computation | async-start | bytes 3145728 | tf_op jit(solution)/shard_map/all_to_all | solution.py:43
  25.6 116.3 %all-gather.2.cloned.1.call-start = ((), (), s32[]{:S(2)}) async-start(), calls=%async_computation.1 | async-start | bytes 3244032 | tf_op jit(solution)/shard_map/all_gather | solution.py:53
  26.5 16.3 %copy-start.4 = (s32[48]{0:T(128)S(1)}, s32[48]{0:T(128)}, u32[]{:S(2)}) copy-start(s32[48]{0:T(128)} %param.16) | copy-start | bytes 580
  56.9 1.2 copy-start.1
  56.9 2.7 %copy-start.3 = (f32[8,6,64]{2,0,1:T(8,128)S(1)}, f32[8,6,64]{2,0,1:T(8,128)}, u32[]{:S(2)}) copy-start(f32[8,6,64]{2,0,1:T(8,128)} %param.12) | copy-start | bytes 36868
Sparse Core Ops, SparseCore 0:
  57.9 83.9 all-gather.1
